TPU v7x, 128 devices: a whole 4x4x4 slice. The times are simulated.
128 devices in a mesh: proj: 16 (over z_lo, y, core), row: 8 (over x, z_hi).
Axes of the slice: x: 4, y: 4, z: 4 (z_hi: 2, z_lo: 2; z = z_hi * 2 + z_lo), core: 2. Of those that a mesh axis runs over, the one named last changes fastest.
Arguments:
- projections: float32 [8192, 8, 1536], P('proj', 'row'), may hold values from -40000 to 40000
Outputs:
- gram: float32 [8192, 8192], P('proj', 'row')
All inputs are finite; a program needn't handle non-finite values.
Results may differ from a plain program's by a relative error of at most 0.0017.
Values may be sent and summed in bfloat16 or wider, within the bound.
A program may use at most 128 MiB of HBM per device.

v0:
```python
import math

import jax
import jax.numpy as jnp
from jax import lax
from jax.sharding import PartitionSpec as P


def per_device(projections):
    tile_rows, det_rows, columns = projections.shape
    entries = det_rows * lax.axis_size("row") * columns
    filtered = projections - jnp.mean(projections, axis=2, keepdims=True)
    energy = lax.psum(jnp.sum(filtered * filtered, axis=(1, 2)), "row")
    band_power = energy / entries
    normed = (
        filtered * lax.rsqrt(band_power + 1e-05)[:, None, None] * (1.0 / math.sqrt(entries))
    ).astype(jnp.bfloat16)
    flattened = normed.reshape(tile_rows, det_rows * columns)
    contract = (((1,), (1,)), ((), ()))
    product = lax.dot_general(
        flattened,
        lax.all_gather(flattened, "proj", axis=0, tiled=True),
        contract,
        preferred_element_type=jnp.float32,
    )
    return lax.psum_scatter(product, "row", scatter_dimension=1, tiled=True)


def solution(mesh):
    in_specs = (P("proj", "row", None),)
    out_specs = P("proj", "row")
    return jax.shard_map(
        per_device, mesh=mesh, in_specs=in_specs, out_specs=out_specs, check_vma=False
    )
```

profile of v0, /device:TPU:17, one launch (start us, length us, event | category | flops | bytes accessed | tf_op | source)
XLA Modules:
  0.0 386.3 jit_solution(17753626626749477230)
XLA Ops:
  6.5 0.0 copy-start
  6.5 0.0 all-gather.3.cloned.1.call-start
  6.5 4.2 %reduce_sum.18 = f32[512]{0:T(512)S(1)} reduce(f32[512,1,1536]{2,1,0:T(1,128)} %param.1, f32[]{:T(128)} %constant.2.clone.1), dimensions={1,2}, to_apply=%region_0.0 | reduce | flops 785920 | bytes 3147780 | tf_op jit(solution)/shard_map/reduce_sum | solution.py:12
  10.8 0.0 copy-done
  10.8 0.4 multiply_reduce_fusion
  11.3 21.3 %psum.7 = f32[512]{0:T(512)S(1)} all-reduce(f32[512]{0:T(512)S(1)} %multiply_reduce_fusion), channel_id=1, replica_groups=mesh['proj'=16,'row'=8] {'row'}, use_global_device_ids=true, to_apply=%region_2.0 | all-reduce | flops 512 | bytes 4096 | tf_op jit(solution)/shard_map/psum | solution.py:13
  32.5 1.6 multiply_convert_fusion
  34.1 0.0 all-gather.3.cloned.1.call-update
  34.2 0.0 reduce-scatter.2.cloned.1.call-start
  34.2 131.5 %all-gather.3.cloned.1.call-done = bf16[8192,1,1536]{2,0,1:T(8,128)(2,1)} async-done(((bf16[512,1,1536]{2,0,1:T(8,128)(2,1)}), bf16[8192,1,1536]{2,0,1:T(8,128)(2,1)}) %all-gather.3.cloned.1.call-update) | async-done | bytes 25165840 | tf_op jit(solution)/shard_map/all_gather | solution.py:22
  165.7 20.8 %fusion = f32[512,8192]{1,0:T(8,128)} fusion(bf16[8192,1,1536]{2,0,1:T(8,128)(2,1)} %all-gather.3.cloned.1.call-done, bf16[512,1,1536]{2,0,1:T(8,128)(2,1)} %multiply_convert_fusion), kind=kOutput, calls=%fused_computation | convolution fusion | flops 12884901888 | bytes 43515904 | tf_op jit(solution)/shard_map/dot_general | solution.py:20
  186.5 0.0 reduce-scatter.2.cloned.1.call-update
  186.5 192.9 %reduce-scatter.2.cloned.1.call-done = f32[512,1024]{1,0:T(8,128)} async-done(((f32[512,8192]{1,0:T(8,128)}), f32[512,1024]{1,0:T(8,128)}) %reduce-scatter.2.cloned.1.call-update) | async-done | bytes 2097168 | tf_op jit(solution)/shard_map/reduce_scatter | solution.py:26
  (2 shorter events, 0.0 us)
Async XLA Ops:
  6.5 4.3 %copy-start = (f32[512,1,1536]{2,1,0:T(1,128)S(1)}, f32[512,1,1536]{2,1,0:T(1,128)}, u32[]{:S(2)}) copy-start(f32[512,1,1536]{2,1,0:T(1,128)} %param.1) | copy-start | bytes 9437188
  6.5 159.2 %all-gather.3.cloned.1.call-start = ((), (), s32[]{:S(2)}) async-start(), calls=%async_computation.2 | async-start | bytes 26738688 | tf_op jit(solution)/shard_map/all_gather | solution.py:22
  34.2 345.2 %reduce-scatter.2.cloned.1.call-start = ((), (), s32[]{:S(2)}) async-start(), calls=%async_computation.1 | async-start | bytes 18874368 | tf_op jit(solution)/shard_map/reduce_scatter | solution.py:26
Sparse Core Ops, SparseCore 0:
  34.3 131.3 all-gather.2
  186.7 192.7 reduce-scatter.1
where the time goes:
time: 389 us; the launch traced here: 386 us
  waiting for transfers between devices  324 us (83%)
  blocking collectives  21.3 us (5%)
  matrix products  20.8 us (5%)
  between operations  13.4 us (3%)
  other arithmetic  6.33 us (2%)
    reduce_scatter x1, waiting for transfers between devices, per_device(): return lax.psum_scatter(product, 'row', scatter_dimension=1, tiled=True)  193 us
    all_gather x1, waiting for transfers between devices, per_device(): lax.all_gather(flattened, 'proj', axis=0, tiled=True)  131 us
    psum x1, blocking collectives, per_device(): energy = lax.psum(jnp.sum(filtered * filtered, axis=(1, 2)), 'row')  21.3 us
    dot_general x1, matrix products, per_device(): lax.dot_general(flattened, lax.all_gather(flattened, 'proj', axis=0, tile...  20.8 us
  transfers between devices with their start and end apart: 2, of which 2 were waited for; matrix products, arithmetic and copies ran while one was open for 0% of the time, Pallas kernels for 0%

commit v1 on v0

v1 whole, which is shorter than its diff:
```python
import functools
import math

import jax
import jax.numpy as jnp
from jax import lax
from jax.experimental import pallas as pl
from jax.experimental.pallas import tpu as pltpu
from jax.sharding import PartitionSpec as P

MESH = pl.DeviceIdType.MESH
CH = 64
TB = 128


def kernel(entries, x_ref, o_ref, xf, mine, sums, pbuf, qbuf, acc, ra, rb, fp, fm, sem_sum, sem_z, sem_n, sem_m, sem_yn,
           sem_ym, sem_c, sem_l, sem_rs):
    rows, cols = x_ref.shape
    nt = rows // TB
    nc = rows // CH
    p, r = lax.axis_index("proj"), lax.axis_index("row")
    zl, y, c = p // 8, (p // 2) % 4, p % 2
    x, zh = r // 2, r % 2
    z = 2 * zh + zl

    def dev(x, y, z, c):
        return ((z % 2) * 8 + y * 2 + c, x * 2 + z // 2)

    k = x // 2
    src = ((x + 1) // 2) % 2 == zl
    ysrc = y // 2 == x % 2
    d_z = dev(x, y, z + 1 - 2 * zl, c)
    d_n = dev(x + 1 - 2 * (x % 2), y, z, c)
    d_m = dev(3 - x, y, z, c)
    d_yn = dev(x, 3 - y, z, c)
    d_ym = dev(x, y + 1 - 2 * (y % 2), z, c)
    d_c = dev(x, y, z, 1 - c)
    d_up = dev(x, y, (z + 1) % 4, c)
    d_dn = dev(x, y, (z + 3) % 4, c)
    peers = [(p, (r + s) % 8) for s in range(1, 8)]

    barrier = pltpu.get_barrier_semaphore()
    for d in peers + [d_up, d_dn, d_yn, d_ym, d_c]:
        pl.semaphore_signal(barrier, inc=1, device_id=d, device_id_type=MESH)

    def copy(source, target, sem, index, device):
        return pltpu.make_async_remote_copy(
            src_ref=source, dst_ref=target, send_sem=sem.at[(0, *index)], recv_sem=sem.at[(1, *index)],
            device_id=device, device_id_type=MESH)

    for q in range(nt):
        part = x_ref[q * TB:(q + 1) * TB, :]
        part = part - jnp.sum(part, axis=1, keepdims=True) * (1.0 / cols)
        xf[q * TB:(q + 1) * TB, :] = part
        square = part[:, :128] * part[:, :128]
        for s in range(1, cols // 128):
            lanes = part[:, s * 128:(s + 1) * 128]
            square = square + lanes * lanes
        mine[q:q + 1, :] = jnp.sum(square.T, axis=0, keepdims=True)
    mine[nt:, :] = jnp.zeros((8 - nt, 128), jnp.float32)
    pl.semaphore_wait(barrier, 12)
    for s, d in enumerate(peers):
        copy(mine, sums.at[r], sem_sum, (s,), d).start()
    total = mine[...]
    for s, d in enumerate(peers):
        copy(mine, sums.at[(r + 7 - s) % 8], sem_sum, (s,), d).wait_recv()
        total = total + sums[(r + 7 - s) % 8]
    scale = lax.rsqrt(total * (1.0 / entries) + 1e-05) * (1.0 / math.sqrt(entries))

    def at(t):
        return t * CH // TB, pl.ds(t * CH % TB, CH)

    def pslot(slot, t):
        chunk, span = at(t)
        return pbuf.at[slot, chunk, span]

    def qslot(j, kk, half, t):
        chunk, span = at(t)
        return qbuf.at[j, kk, chunk, half, span]

    def c_z(t):
        return copy(pslot(4, t), pslot(2 * k + zl, t), sem_z, (t,), d_z)

    def c_n(t, i):
        return copy(pslot(2 * k + i, t), pslot(2 * k + i, t), sem_n, (t, i), d_n)

    def c_m(t, i):
        return copy(pslot(2 * k + i, t), pslot(2 * k + i, t), sem_m, (t, i), d_m)

    def start_native(t):
        c_n(t, zl).start()
        c_m(t, zl).start()

    native = jnp.where(src, 2 * k + zl, 4)
    for q in range(nt):
        spread = jnp.broadcast_to(scale[q:q + 1, :], (128, 128)).T
        for s in range(cols // 128):
            lanes = slice(s * 128, (s + 1) * 128)
            pbuf[native, q, :, lanes] = (xf[q * TB:(q + 1) * TB, lanes] * spread).astype(jnp.bfloat16)

        @pl.when(jnp.logical_not(src))
        def _():
            for t in range(q * TB // CH, (q + 1) * TB // CH):
                c_z(t).start()

        if q == 0:
            @pl.when(src)
            def _():
                start_native(0)

    def s1(t):
        @pl.when(src)
        def _():
            if t + 1 < nc:
                start_native(t + 1)
            copy(pslot(4, t), pslot(2 * k + 1 - zl, t), sem_z, (t,), d_z).wait_recv()
            c_n(t, 1 - zl).start()
            c_m(t, 1 - zl).start()

    def s2(t):
        @pl.when(jnp.logical_not(src))
        def _():
            for i in (zl, 1 - zl):
                c_n(t, i).wait_recv()
                c_m(t, i).start()

    def c_yn(t, kk):
        return copy(pslot(2 * kk + k, t), qslot(y % 2, kk, c, t), sem_yn, (t, kk), d_yn)

    def c_ym_source(t, kk):
        return copy(pslot(2 * kk + k, t), qslot(y % 2, kk, c, t), sem_ym, (t, kk), d_ym)

    def c_ym_other(t, kk):
        slot = qslot(1 - y % 2, kk, c, t)
        return copy(slot, slot, sem_ym, (t, kk), d_ym)

    def c_c_source(t, kk):
        return copy(pslot(2 * kk + k, t), qslot(y % 2, kk, c, t), sem_c, (t, y % 2, kk), d_c)

    def c_c(t, j, kk):
        return copy(qslot(j, kk, c, t), qslot(j, kk, c, t), sem_c, (t, j, kk), d_c)

    def c_l(t, kk):
        return pltpu.make_async_copy(pslot(2 * kk + k, t), qslot(y % 2, kk, c, t), sem_l.at[t, kk])

    def s3(t):
        for i in range(2):
            copy(pslot(2 * (1 - k) + i, t), pslot(2 * (1 - k) + i, t), sem_m, (t, i), d_m).wait_recv()

        @pl.when(ysrc)
        def _():
            for kk in range(2):
                c_yn(t, kk).start()
                c_ym_source(t, kk).start()
                c_c_source(t, kk).start()
                c_l(t, kk).start()

    def s4(t):
        @pl.when(jnp.logical_not(ysrc))
        def _():
            for kk in range(2):
                slot = qslot(1 - y % 2, kk, c, t)
                copy(slot, slot, sem_yn, (t, kk), d_yn).wait_recv()
                c_ym_other(t, kk).start()
                c_c(t, 1 - y % 2, kk).start()

    from_mate = jnp.where(ysrc, 1 - y % 2, y % 2)

    def s5(t):
        for kk in range(2):
            slot = qslot(from_mate, kk, c, t)
            copy(slot, slot, sem_ym, (t, kk), d_ym).wait_recv()
            c_c(t, from_mate, kk).start()

    def s6(t):
        for kk in range(2):
            for j in range(2):
                slot = qslot(j, kk, 1 - c, t)
                copy(slot, slot, sem_c, (t, j, kk), d_c).wait_recv()

        @pl.when(ysrc)
        def _():
            for kk in range(2):
                c_l(t, kk).wait()

    owners = [(z + 2) % 4, (z + 3) % 4, (z + 1) % 4, z]

    def multiply(e, t):
        i, j = owners[e] % 2, owners[e] // 2

        def unit(u, carry):
            tp = jnp.where(u <= t, t, u - t - 1)
            tq = jnp.where(u <= t, u, t)
            out = None
            for kk in range(2):
                part = lax.dot_general(
                    pbuf[2 * kk + i, tp], qbuf[j, kk, tq].reshape(2 * TB, cols), (((1,), (1,)), ((), ())),
                    preferred_element_type=jnp.float32)
                out = part if out is None else out + part
            acc[e, 0, tp, tq] = out[:, :TB]
            acc[e, 1, tp, tq] = out[:, TB:]
            return carry

        lax.fori_loop(0, 2 * t + 1, unit, 0)

    def rects(t):
        first = [(max(2 * t - 1, 0), (t, pl.ds(0, t + 1)))]
        return first + ([(2 * t, (pl.ds(0, t), t))] if t else [])

    def region(buf, lead, index):
        return buf.at[(*lead, *index)]

    RA, RB, FP0, FP1, FM0, FM1 = range(6)

    def c_rs(kind, n, index):
        source, lead, target, tlead, device = {
            RA: (acc, (0, 0), ra, (), d_dn),
            RB: (acc, (0, 1), rb, (), d_up),
            FP0: (acc, (1, 0), fp, (0,), d_dn),
            FP1: (acc, (1, 1), fp, (1,), d_dn),
            FM0: (acc, (2, 0), fm, (0,), d_up),
            FM1: (acc, (2, 1), fm, (1,), d_up),
        }[kind]
        return copy(region(source, lead, index), region(target, tlead, index), sem_rs, (kind, n), device)

    def relay(t):
        for kind, e, h, buf, onward in ((RA, 1, 0, ra, FP0), (RB, 2, 1, rb, FM1)):
            for n, index in rects(t):
                c_rs(kind, n, index).wait_recv()
                here = (e, h, *index)
                acc[here] = acc[here] + buf[index]
                c_rs(onward, n, index).start()

    def compute(t):
        multiply(0, t)
        for n, index in rects(t):
            c_rs(RA, n, index).start()
            c_rs(RB, n, index).start()
        multiply(1, t)
        for n, index in rects(t):
            c_rs(FP1, n, index).start()
        multiply(2, t)
        for n, index in rects(t):
            c_rs(FM0, n, index).start()
        if t:
            relay(t - 1)
        multiply(3, t)

    for tick in range(nc + 2):
        if tick < nc:
            s1(tick)
            s2(tick)
        if tick >= 2:
            s5(tick - 2)
        if tick < nc:
            s3(tick)
        if tick >= 2:
            s6(tick - 2)
        if 0 <= tick - 1 < nc:
            s4(tick - 1)
        if tick >= 2 and (tick - 1) * CH % TB == 0:
            compute((tick - 1) * CH // TB - 1)
    relay(nt - 1)

    for t in range(nt):
        for n, index in rects(t):
            for kind in (FP0, FP1, FM0, FM1):
                c_rs(kind, n, index).wait_recv()
    for tp in range(nt):
        for h in range(2):
            for tq in range(nt):
                lanes = slice((h * nt + tq) * TB, (h * nt + tq + 1) * TB)
                o_ref[tp * TB:(tp + 1) * TB, lanes] = acc[3, h, tp, tq] + fp[h, tp, tq] + fm[h, tp, tq]

    for s, d in enumerate(peers):
        copy(mine, sums.at[r], sem_sum, (s,), d).wait_send()
    for t in range(nc):
        @pl.when(src)
        def _():
            for i in range(2):
                c_n(t, i).wait_send()

        @pl.when(jnp.logical_not(src))
        def _():
            c_z(t).wait_send()

        for i in range(2):
            c_m(t, i).wait_send()
        for kk in range(2):
            @pl.when(ysrc)
            def _():
                c_yn(t, kk).wait_send()

            c_ym_other(t, kk).wait_send()
            for j in range(2):
                c_c(t, j, kk).wait_send()
    for t in range(nt):
        for n, index in rects(t):
            for kind in range(6):
                c_rs(kind, n, index).wait_send()


def per_device(projections):
    rows, _, cols = projections.shape
    entries = 8 * cols
    nt, nc = rows // TB, rows // CH
    nr = 2 * nt - 1
    dma = pltpu.SemaphoreType.DMA
    return pl.pallas_call(
        functools.partial(kernel, entries),
        out_shape=jax.ShapeDtypeStruct((rows, 2 * rows), jnp.float32),
        in_specs=[pl.BlockSpec(memory_space=pltpu.VMEM)],
        out_specs=pl.BlockSpec(memory_space=pltpu.VMEM),
        scratch_shapes=[
            pltpu.VMEM((rows, cols), jnp.float32),
            pltpu.VMEM((8, 128), jnp.float32),
            pltpu.VMEM((8, 8, 128), jnp.float32),
            pltpu.VMEM((5, nt, TB, cols), jnp.bfloat16),
            pltpu.VMEM((2, 2, nt, 2, TB, cols), jnp.bfloat16),
            pltpu.VMEM((4, 2, nt, nt, TB, TB), jnp.float32),
            pltpu.VMEM((nt, nt, TB, TB), jnp.float32),
            pltpu.VMEM((nt, nt, TB, TB), jnp.float32),
            pltpu.VMEM((2, nt, nt, TB, TB), jnp.float32),
            pltpu.VMEM((2, nt, nt, TB, TB), jnp.float32),
            dma((2, 7)),
            dma((2, nc)),
            dma((2, nc, 2)),
            dma((2, nc, 2)),
            dma((2, nc, 2)),
            dma((2, nc, 2)),
            dma((2, nc, 2, 2)),
            dma((nc, 2)),
            dma((2, 6, nr)),
        ],
        compiler_params=pltpu.CompilerParams(
            collective_id=0, has_side_effects=True, vmem_limit_bytes=60 * 2**20
        ),
    )(projections.reshape(rows, cols))


def solution(mesh):
    return jax.shard_map(
        per_device, mesh=mesh, in_specs=(P("proj", "row", None),), out_specs=P("proj", "row"), check_vma=False
    )
```

time: 389 us -> 200 us (0.51)
  waiting for transfers between devices: 324 us -> 0 us
  Pallas kernels: 0 us -> 193 us
  blocking collectives: 21.3 us -> 0 us
  matrix products: 20.8 us -> 0 us
  between operations: 13.4 us -> 0.01 us
  local copies, waits for them, and re-layouts: 0.01 us -> 6.92 us
  other arithmetic: 6.33 us -> 0 us
    reduce_scatter x1 -> x0, waiting for transfers between devices: 193 us -> none  [per_device(): return lax.psum_scatter(product, 'row', scatter_dimension=1, tiled=True)]
    pallas_call x0 -> x1, Pallas kernels: none -> 193 us  [per_device(): pl.pallas_call(functools.partial(kernel, entries), out_shape=jax.ShapeDty...]
    all_gather x1 -> x0, waiting for transfers between devices: 131 us -> none  [per_device(): lax.all_gather(flattened, 'proj', axis=0, tiled=True)]
    psum x1 -> x0, blocking collectives: 21.3 us -> none  [per_device(): energy = lax.psum(jnp.sum(filtered * filtered, axis=(1, 2)), 'row')]
    dot_general x1 -> x0, matrix products: 20.8 us -> none  [per_device(): lax.dot_general(flattened, lax.all_gather(flattened, 'proj', axis=0, tile...]
    unnamed x2, local copies, waits for them, and re-layouts: 0.01 us -> 6.92 us
    reduce_sum x2 -> x0, other arithmetic: 4.7 us -> none  [the longest x1 4.25 us: per_device(): filtered = projections - jnp.mean(projections, axis=2, keepdims=True)]
  transfers between devices with their start and end apart: 2 -> 0, of which waited for: 2 -> 0; matrix products, arithmetic and copies ran while one was open for 0% -> 0% of each run, Pallas kernels for 0% -> 0%
where the time goes in v1:
time: 200 us
  Pallas kernels  193 us (96%)
  local copies, waits for them, and re-layouts  6.92 us (3%)
    pallas_call x1, Pallas kernels, per_device(): pl.pallas_call(functools.partial(kernel, entries), out_shape=jax.ShapeDty...  193 us
    unnamed x2, local copies, waits for them, and re-layouts  6.92 us

profile of v1, /device:TPU:17, one launch (start us, length us, event | category | flops | bytes accessed | tf_op | source)
XLA Modules:
  0.0 199.6 jit_solution(13690618820076227981)
XLA Ops:
  0.0 3.8 %copy.4 = f32[512,1,1536]{2,0,1:T(8,128)} copy(f32[512,1,1536]{2,1,0:T(1,128)} %param.1) | data formatting | bytes 6291456
  3.8 192.7 %shard_map.17 = f32[512,1024]{1,0:T(8,128)} custom-call(f32[512,1536]{1,0:T(8,128)} %bitcast.3), custom_call_target="tpu_custom_call" | custom-call | tf_op jit(solution)/shard_map/pallas_call | solution.py:309
  196.5 3.2 %copy.6 = f32[512,1024]{1,0:T(8,128)} copy(f32[512,1024]{1,0:T(8,128)} %shard_map.17) | data formatting | bytes 4194304

commit v2 on v1

v2 whole, which is shorter than its diff:
```python
import functools
import math

import jax
import jax.numpy as jnp
from jax import lax
from jax.experimental import pallas as pl
from jax.experimental.pallas import tpu as pltpu
from jax.sharding import PartitionSpec as P

MESH = pl.DeviceIdType.MESH
CH = 64
TB = 128
RB = 256
ORDER = [
    ("2a", 0), ("2a", 1), ("1", 0), ("3o", 0), ("3a", 0), ("1", 1), ("3o", 1), ("3a", 1), ("2a", 2), ("2a", 3),
    ("1", 2), ("1", 3), ("3a", 2), ("3o", 2), ("1", 4), ("4", 0), ("1", 5), ("3a", 3), ("2a", 4), ("2a", 5), ("4", 1),
    ("2a", 6), ("2a", 7), ("3o", 3), ("1", 6), ("3a", 4), ("1", 7), ("4", 2), ("3o", 4), ("2b", 0), ("3o", 5),
    ("1n", 0), ("3a", 5), ("3a", 6), ("5", 0), ("6", 0), ("2b", 1), ("3o", 6), ("5", 1), ("6", 1), ("C", (0, 0, 0)),
    ("R", (0, 0, 0)), ("4", 3), ("2b", 2), ("2b", 3), ("3a", 7), ("C", (0, 0, 1)), ("3b", 0), ("2b", 4),
    ("R", (0, 0, 1)), ("3b", 1), ("3b", 2), ("4", 4), ("3b", 3), ("C", (1, 0, 0)), ("5", 2), ("6", 2), ("5", 3),
    ("6", 3), ("2b", 5), ("C", (1, 1, 0)), ("2b", 6), ("C", (0, 1, 0)), ("C", (0, 1, 1)), ("R", (0, 1, 0)), ("2b", 7),
    ("R", (1, 0, 0)), ("R", (0, 1, 1)), ("3b", 4), ("3b", 5), ("4", 5), ("R", (1, 1, 0)), ("3o", 7), ("3b", 6),
    ("3b", 7), ("C", (1, 1, 1)), ("C", (1, 0, 1)), ("4", 6), ("5", 4), ("5", 5), ("6", 4), ("6", 5), ("C", (1, 2, 1)),
    ("C", (1, 2, 0)), ("C", (0, 2, 0)), ("F", (1, 0)), ("4", 7), ("R", (0, 2, 0)), ("R", (1, 0, 1)), ("F", (0, 0)),
    ("5", 6), ("6", 6), ("F", (0, 1)), ("C", (0, 2, 1)), ("F", (1, 1)), ("R", (1, 1, 1)), ("R", (0, 2, 1)),
    ("R", (1, 2, 0)), ("R", (1, 2, 1)), ("5", 7), ("6", 7), ("C", (0, 3, 0)), ("C", (1, 3, 0)), ("C", (1, 3, 1)),
    ("R", (0, 3, 0)), ("C", (0, 3, 1)), ("R", (0, 3, 1)), ("F", (2, 1)), ("R", (1, 3, 1)), ("R", (1, 3, 0)),
    ("F", (2, 0)), ("F", (3, 0)), ("F", (3, 1)),
]


def kernel(entries, x_hbm, o_ref, x_ref, sem_x, xf, mine, sums, pbuf, qbuf, acc, ra, rb, fp, fm, sem_sum, sem_z, sem_n, sem_m, sem_yn,
           sem_ym, sem_c, sem_l, sem_rs):
    rows, cols = x_ref.shape
    nt = rows // TB
    nc = rows // CH
    p, r = lax.axis_index("proj"), lax.axis_index("row")
    zl, y, c = p // 8, (p // 2) % 4, p % 2
    x, zh = r // 2, r % 2
    z = 2 * zh + zl

    def dev(x, y, z, c):
        return ((z % 2) * 8 + y * 2 + c, x * 2 + z // 2)

    k = x // 2
    src = ((x + 1) // 2) % 2 == zl
    ysrc = y // 2 == x % 2
    d_z = dev(x, y, z + 1 - 2 * zl, c)
    d_n = dev(x + 1 - 2 * (x % 2), y, z, c)
    d_m = dev(3 - x, y, z, c)
    d_yn = dev(x, 3 - y, z, c)
    d_ym = dev(x, y + 1 - 2 * (y % 2), z, c)
    d_c = dev(x, y, z, 1 - c)
    d_up = dev(x, y, (z + 1) % 4, c)
    d_dn = dev(x, y, (z + 3) % 4, c)
    peers = [(p, (r + s) % 8) for s in range(1, 8)]

    def load(q):
        span = pl.ds(q * TB, TB)
        return pltpu.make_async_copy(x_hbm.at[span, 0, :], x_ref.at[span, :], sem_x.at[q])

    for q in range(nt):
        load(q).start()
    barrier = pltpu.get_barrier_semaphore()
    for d in peers + [d_up, d_dn, d_yn, d_ym, d_c]:
        pl.semaphore_signal(barrier, inc=1, device_id=d, device_id_type=MESH)

    def copy(source, target, sem, index, device):
        return pltpu.make_async_remote_copy(
            src_ref=source, dst_ref=target, send_sem=sem.at[(0, *index)], recv_sem=sem.at[(1, *index)],
            device_id=device, device_id_type=MESH)

    for q in range(nt):
        load(q).wait()
        part = x_ref[q * TB:(q + 1) * TB, :]
        part = part - jnp.sum(part, axis=1, keepdims=True) * (1.0 / cols)
        xf[q * TB:(q + 1) * TB, :] = part
        square = part[:, :128] * part[:, :128]
        for s in range(1, cols // 128):
            lanes = part[:, s * 128:(s + 1) * 128]
            square = square + lanes * lanes
        mine[q:q + 1, :] = jnp.sum(square.T, axis=0, keepdims=True)
    mine[nt:, :] = jnp.zeros((8 - nt, 128), jnp.float32)
    pl.semaphore_wait(barrier, 12)
    for s, d in enumerate(peers):
        copy(mine, sums.at[r], sem_sum, (s,), d).start()
    total = mine[...]
    for s, d in enumerate(peers):
        copy(mine, sums.at[(r + 7 - s) % 8], sem_sum, (s,), d).wait_recv()
        total = total + sums[(r + 7 - s) % 8]
    scale = lax.rsqrt(total * (1.0 / entries) + 1e-05) * (1.0 / math.sqrt(entries))

    def at(t):
        return t * CH // TB, pl.ds(t * CH % TB, CH)

    def pslot(slot, t):
        return pbuf.at[slot, t * CH // RB, pl.ds(t * CH % RB, CH)]

    def qslot(j, kk, half, t):
        chunk, span = at(t)
        return qbuf.at[j, kk, chunk, half, span]

    def c_z(t):
        return copy(pslot(4, t), pslot(2 * k + zl, t), sem_z, (t,), d_z)

    def c_n(t, i):
        return copy(pslot(2 * k + i, t), pslot(2 * k + i, t), sem_n, (t, i), d_n)

    def c_m(t, i):
        return copy(pslot(2 * k + i, t), pslot(2 * k + i, t), sem_m, (t, i), d_m)

    first = jnp.where(ysrc, k, 1 - k)

    native = jnp.where(src, 2 * k + zl, 4)
    for q in range(nt):
        spread = jnp.broadcast_to(scale[q:q + 1, :], (128, 128)).T
        rh, span = q * TB // RB, slice(q * TB % RB, q * TB % RB + TB)
        for s in range(cols // 128):
            lanes = slice(s * 128, (s + 1) * 128)
            pbuf[native, rh, span, lanes] = (xf[q * TB:(q + 1) * TB, lanes] * spread).astype(jnp.bfloat16)
        chunks = range(q * TB // CH, (q + 1) * TB // CH)

        @pl.when(jnp.logical_not(src))
        def _():
            for t in chunks:
                c_z(t).start()

        @pl.when(src & (zl == first))
        def _():
            for t in chunks:
                c_m(t, zl).start()

        @pl.when(src & (zl != first))
        def _():
            for t in chunks:
                c_n(t, zl).start()

    def s1(t):
        @pl.when(src)
        def _():
            copy(pslot(4, t), pslot(2 * k + 1 - zl, t), sem_z, (t,), d_z).wait_recv()
            c_n(t, 1 - zl).start()
            c_m(t, 1 - zl).start()

    def s1n(_):
        @pl.when(src & (zl == first))
        def _():
            for t in range(nc):
                c_n(t, zl).start()

        @pl.when(src & (zl != first))
        def _():
            for t in range(nc):
                c_m(t, zl).start()

    def s2(t, i):
        @pl.when(jnp.logical_not(src))
        def _():
            c_n(t, i).wait_recv()
            c_m(t, i).start()

    def c_yn(t, kk):
        return copy(pslot(2 * kk + k, t), qslot(y % 2, kk, c, t), sem_yn, (t, kk), d_yn)

    def c_ym_source(t, kk):
        return copy(pslot(2 * kk + k, t), qslot(y % 2, kk, c, t), sem_ym, (t, kk), d_ym)

    def c_ym_other(t, kk):
        slot = qslot(1 - y % 2, kk, c, t)
        return copy(slot, slot, sem_ym, (t, kk), d_ym)

    def c_c_source(t, kk):
        return copy(pslot(2 * kk + k, t), qslot(y % 2, kk, c, t), sem_c, (t, y % 2, kk), d_c)

    def c_c(t, j, kk):
        return copy(qslot(j, kk, c, t), qslot(j, kk, c, t), sem_c, (t, j, kk), d_c)

    def c_l(t, kk):
        return pltpu.make_async_copy(pslot(2 * kk + k, t), qslot(y % 2, kk, c, t), sem_l.at[t, kk])

    def give(t, kk):
        c_yn(t, kk).start()
        c_ym_source(t, kk).start()
        c_c_source(t, kk).start()
        c_l(t, kk).start()

    def s3o(t):
        @pl.when(ysrc)
        def _():
            give(t, k)

    def s3(t, i):
        slot = pslot(2 * (1 - k) + i, t)
        copy(slot, slot, sem_m, (t, i), d_m).wait_recv()

    def s3a(t):
        s3(t, first)

        @pl.when(ysrc)
        def _():
            give(t, 1 - k)

    def s4(t):
        @pl.when(jnp.logical_not(ysrc))
        def _():
            for kk in (k, 1 - k):
                slot = qslot(1 - y % 2, kk, c, t)
                copy(slot, slot, sem_yn, (t, kk), d_yn).wait_recv()
                c_ym_other(t, kk).start()
                c_c(t, 1 - y % 2, kk).start()

    from_mate = jnp.where(ysrc, 1 - y % 2, y % 2)

    def s5(t):
        for kk in (k, 1 - k):
            slot = qslot(from_mate, kk, c, t)
            copy(slot, slot, sem_ym, (t, kk), d_ym).wait_recv()
            c_c(t, from_mate, kk).start()

    def s6(t):
        for kk in range(2):
            for j in range(2):
                slot = qslot(j, kk, 1 - c, t)
                copy(slot, slot, sem_c, (t, j, kk), d_c).wait_recv()

        @pl.when(ysrc)
        def _():
            for kk in range(2):
                c_l(t, kk).wait()


    def sides(g):
        return (zl != first) if g == 0 else (zl == first)

    def multiply(e, t, rh):
        owner = (z + jnp.where(e < 2, 2 + e, 7 - e)) % 4
        i, j = owner % 2, owner // 2
        out = None
        for kk in range(2):
            part = lax.dot_general(
                pbuf[2 * kk + i, rh], qbuf[j, kk, t].reshape(2 * TB, cols), (((1,), (1,)), ((), ())),
                preferred_element_type=jnp.float32)
            out = part if out is None else out + part
        acc[e, 0, t, rh] = out[:, :TB]
        acc[e, 1, t, rh] = out[:, TB:]

    TO_DN, TO_UP, FP0, FP1, FM0, FM1 = range(6)

    def c_rs(kind, t, rh):
        source, target, device = {
            TO_DN: (acc.at[0, 0, t, rh], ra.at[t, rh], d_dn),
            TO_UP: (acc.at[0, 1, t, rh], rb.at[t, rh], d_up),
            FP0: (acc.at[1, 0, t, rh], fp.at[0, t, rh], d_dn),
            FP1: (acc.at[1, 1, t, rh], fp.at[1, t, rh], d_dn),
            FM0: (acc.at[2, 0, t, rh], fm.at[0, t, rh], d_up),
            FM1: (acc.at[2, 1, t, rh], fm.at[1, t, rh], d_up),
        }[kind]
        return copy(source, target, sem_rs, (kind, t, rh), device)

    def compute(a):
        g, t, rh = a
        side = sides(g).astype(jnp.int32)

        def one(n, carry):
            multiply(3 * n + side * (1 - 2 * n), t, rh)
            return carry

        lax.fori_loop(0, 2, one, 0)

        @pl.when(sides(g))
        def _():
            c_rs(FP1, t, rh).start()
            c_rs(FM0, t, rh).start()

        @pl.when(jnp.logical_not(sides(g)))
        def _():
            c_rs(TO_DN, t, rh).start()
            c_rs(TO_UP, t, rh).start()

    def relay(a):
        g, t, rh = a

        @pl.when(sides(g))
        def _():
            for kind, e, h, buf, onward in ((TO_DN, 1, 0, ra, FP0), (TO_UP, 2, 1, rb, FM1)):
                c_rs(kind, t, rh).wait_recv()
                acc[e, h, t, rh] = acc[e, h, t, rh] + buf[t, rh]
                c_rs(onward, t, rh).start()

    def finish(a):
        t, rh = a
        for kind in (FP0, FP1, FM0, FM1):
            c_rs(kind, t, rh).wait_recv()
        for h in range(2):
            lanes = slice((h * nt + t) * TB, (h * nt + t + 1) * TB)
            o_ref[rh * RB:(rh + 1) * RB, lanes] = acc[3, h, t, rh] + fp[h, t, rh] + fm[h, t, rh]

    stages = {
        "1": s1, "1n": s1n, "2a": lambda t: s2(t, first), "2b": lambda t: s2(t, 1 - first), "3o": s3o, "3a": s3a,
        "3b": lambda t: s3(t, 1 - first), "4": s4, "5": s5, "6": s6, "C": compute, "R": relay, "F": finish,
    }
    for name, argument in ORDER:
        stages[name](argument)

    for s, d in enumerate(peers):
        copy(mine, sums.at[r], sem_sum, (s,), d).wait_send()
    for t in range(nc):
        @pl.when(src)
        def _():
            for i in range(2):
                c_n(t, i).wait_send()

        @pl.when(jnp.logical_not(src))
        def _():
            c_z(t).wait_send()

        for i in range(2):
            c_m(t, i).wait_send()
        for kk in range(2):
            @pl.when(ysrc)
            def _():
                c_yn(t, kk).wait_send()

            c_ym_other(t, kk).wait_send()
            for j in range(2):
                c_c(t, j, kk).wait_send()
    for t in range(nt):
        for rh in range(2):
            for kind in range(6):
                c_rs(kind, t, rh).wait_send()


def per_device(projections):
    rows, _, cols = projections.shape
    entries = 8 * cols
    nt, nc = rows // TB, rows // CH
    dma = pltpu.SemaphoreType.DMA
    return pl.pallas_call(
        functools.partial(kernel, entries),
        out_shape=jax.ShapeDtypeStruct((rows, 2 * rows), jnp.float32),
        in_specs=[pl.BlockSpec(memory_space=pl.ANY)],
        out_specs=pl.BlockSpec(memory_space=pltpu.VMEM),
        scratch_shapes=[
            pltpu.VMEM((rows, cols), jnp.float32),
            dma((nt,)),
            pltpu.VMEM((rows, cols), jnp.float32),
            pltpu.VMEM((8, 128), jnp.float32),
            pltpu.VMEM((8, 8, 128), jnp.float32),
            pltpu.VMEM((5, rows // RB, RB, cols), jnp.bfloat16),
            pltpu.VMEM((2, 2, nt, 2, TB, cols), jnp.bfloat16),
            pltpu.VMEM((4, 2, nt, rows // RB, RB, TB), jnp.float32),
            pltpu.VMEM((nt, rows // RB, RB, TB), jnp.float32),
            pltpu.VMEM((nt, rows // RB, RB, TB), jnp.float32),
            pltpu.VMEM((2, nt, rows // RB, RB, TB), jnp.float32),
            pltpu.VMEM((2, nt, rows // RB, RB, TB), jnp.float32),
            dma((2, 7)),
            dma((2, nc)),
            dma((2, nc, 2)),
            dma((2, nc, 2)),
            dma((2, nc, 2)),
            dma((2, nc, 2)),
            dma((2, nc, 2, 2)),
            dma((nc, 2)),
            dma((2, 6, nt, rows // RB)),
        ],
        compiler_params=pltpu.CompilerParams(
            collective_id=0, has_side_effects=True, vmem_limit_bytes=60 * 2**20
        ),
    )(projections)


def solution(mesh):
    return jax.shard_map(
        per_device, mesh=mesh, in_specs=(P("proj", "row", None),), out_specs=P("proj", "row"), check_vma=False
    )
```

time: 200 us -> 148 us (0.74)
  Pallas kernels: 193 us -> 144 us
  local copies, waits for them, and re-layouts: 6.92 us -> 3.16 us
    pallas_call x1, Pallas kernels: 193 us -> 144 us  [per_device(): pl.pallas_call(functools.partial(kernel, entries), out_shape=jax.ShapeDty...]
    unnamed x2 -> x1, local copies, waits for them, and re-layouts: 6.92 us -> 3.16 us
where the time goes in v2:
time: 148 us; the launch traced here: 147 us
  Pallas kernels  144 us (97%)
  local copies, waits for them, and re-layouts  3.16 us (2%)
    pallas_call x1, Pallas kernels, per_device(): pl.pallas_call(functools.partial(kernel, entries), out_shape=jax.ShapeDty...  144 us
    unnamed x1, local copies, waits for them, and re-layouts  3.16 us

profile of v2, /device:TPU:17, one launch (start us, length us, event | category | flops | bytes accessed | tf_op | source)
XLA Modules:
  0.0 147.2 jit_solution(15427468702248224702)
XLA Ops:
  0.0 144.0 %shard_map.17 = f32[512,1024]{1,0:T(8,128)} custom-call(f32[512,1,1536]{2,1,0:T(1,128)} %x_hbm.1), custom_call_target="tpu_custom_call" | custom-call | tf_op jit(solution)/shard_map/pallas_call | solution.py:339
  144.0 3.2 %copy.3 = f32[512,1024]{1,0:T(8,128)} copy(f32[512,1024]{1,0:T(8,128)} %shard_map.17) | data formatting | bytes 4194304

commit v3 on v2

--- a/solution.py
+++ b/solution.py
@@ -13,24 +13,24 @@
 TB = 128
 RB = 256
 ORDER = [
-    ("2a", 0), ("2a", 1), ("1", 0), ("3o", 0), ("3a", 0), ("1", 1), ("3o", 1), ("3a", 1), ("2a", 2), ("2a", 3),
-    ("1", 2), ("1", 3), ("3a", 2), ("3o", 2), ("1", 4), ("4", 0), ("1", 5), ("3a", 3), ("2a", 4), ("2a", 5), ("4", 1),
-    ("2a", 6), ("2a", 7), ("3o", 3), ("1", 6), ("3a", 4), ("1", 7), ("4", 2), ("3o", 4), ("2b", 0), ("3o", 5),
-    ("1n", 0), ("3a", 5), ("3a", 6), ("5", 0), ("6", 0), ("2b", 1), ("3o", 6), ("5", 1), ("6", 1), ("C", (0, 0, 0)),
-    ("R", (0, 0, 0)), ("4", 3), ("2b", 2), ("2b", 3), ("3a", 7), ("C", (0, 0, 1)), ("3b", 0), ("2b", 4),
-    ("R", (0, 0, 1)), ("3b", 1), ("3b", 2), ("4", 4), ("3b", 3), ("C", (1, 0, 0)), ("5", 2), ("6", 2), ("5", 3),
-    ("6", 3), ("2b", 5), ("C", (1, 1, 0)), ("2b", 6), ("C", (0, 1, 0)), ("C", (0, 1, 1)), ("R", (0, 1, 0)), ("2b", 7),
-    ("R", (1, 0, 0)), ("R", (0, 1, 1)), ("3b", 4), ("3b", 5), ("4", 5), ("R", (1, 1, 0)), ("3o", 7), ("3b", 6),
-    ("3b", 7), ("C", (1, 1, 1)), ("C", (1, 0, 1)), ("4", 6), ("5", 4), ("5", 5), ("6", 4), ("6", 5), ("C", (1, 2, 1)),
-    ("C", (1, 2, 0)), ("C", (0, 2, 0)), ("F", (1, 0)), ("4", 7), ("R", (0, 2, 0)), ("R", (1, 0, 1)), ("F", (0, 0)),
-    ("5", 6), ("6", 6), ("F", (0, 1)), ("C", (0, 2, 1)), ("F", (1, 1)), ("R", (1, 1, 1)), ("R", (0, 2, 1)),
-    ("R", (1, 2, 0)), ("R", (1, 2, 1)), ("5", 7), ("6", 7), ("C", (0, 3, 0)), ("C", (1, 3, 0)), ("C", (1, 3, 1)),
-    ("R", (0, 3, 0)), ("C", (0, 3, 1)), ("R", (0, 3, 1)), ("F", (2, 1)), ("R", (1, 3, 1)), ("R", (1, 3, 0)),
-    ("F", (2, 0)), ("F", (3, 0)), ("F", (3, 1)),
+    ("2a", 0), ("1", 0), ("3o", 0), ("1", 1), ("2a", 1), ("2a", 2), ("1", 2), ("3a", 0), ("2a", 3), ("1", 3),
+    ("3o", 1), ("3a", 1), ("2a", 4), ("4", 0), ("3o", 2), ("2a", 5), ("2a", 6), ("1", 4), ("1", 5), ("4", 1),
+    ("5", 0), ("3a", 2), ("3a", 3), ("3o", 3), ("2a", 7), ("3a", 4), ("3o", 4), ("1", 6), ("2b", 0), ("1", 7),
+    ("5", 1), ("1n", 0), ("6", 0), ("4", 2), ("3a", 5), ("6", 1), ("C", (0, 0, 0)), ("3o", 5), ("3o", 6),
+    ("R", (0, 0, 0)), ("3a", 6), ("3a", 7), ("2b", 1), ("2b", 2), ("4", 3), ("C", (0, 0, 1)), ("2b", 3), ("3b", 0),
+    ("2b", 4), ("3b", 1), ("R", (0, 0, 1)), ("3b", 2), ("3b", 3), ("C", (1, 0, 0)), ("5", 2), ("2b", 5), ("4", 4),
+    ("6", 2), ("3o", 7), ("5", 3), ("6", 3), ("C", (1, 1, 0)), ("C", (0, 1, 0)), ("C", (0, 1, 1)), ("3b", 4),
+    ("2b", 6), ("2b", 7), ("R", (0, 1, 1)), ("4", 5), ("R", (1, 0, 0)), ("3b", 5), ("3b", 6), ("R", (1, 1, 0)),
+    ("5", 4), ("4", 6), ("R", (0, 1, 0)), ("3b", 7), ("C", (1, 0, 1)), ("C", (1, 1, 1)), ("6", 4), ("5", 5), ("6", 5),
+    ("C", (1, 2, 1)), ("C", (0, 2, 0)), ("F", (0, 0)), ("C", (1, 2, 0)), ("R", (1, 0, 1)), ("C", (0, 2, 1)),
+    ("R", (1, 1, 1)), ("4", 7), ("F", (1, 0)), ("R", (1, 2, 0)), ("5", 6), ("R", (0, 2, 1)), ("6", 6), ("5", 7),
+    ("6", 7), ("R", (0, 2, 0)), ("C", (1, 3, 0)), ("C", (0, 3, 0)), ("C", (1, 3, 1)), ("C", (0, 3, 1)),
+    ("R", (0, 3, 1)), ("R", (0, 3, 0)), ("F", (0, 1)), ("F", (2, 1)), ("R", (1, 2, 1)), ("R", (1, 3, 0)),
+    ("F", (1, 1)), ("R", (1, 3, 1)), ("F", (2, 0)), ("F", (3, 0)), ("F", (3, 1)),
 ]
 
 
-def kernel(entries, x_hbm, o_ref, x_ref, sem_x, xf, mine, sums, pbuf, qbuf, acc, ra, rb, fp, fm, sem_sum, sem_z, sem_n, sem_m, sem_yn,
+def kernel(entries, x_hbm, o_hbm, x_ref, sem_x, o_ref, sem_o, xf, mine, sums, pbuf, qbuf, acc, ra, rb, fp, fm, sem_sum, sem_z, sem_n, sem_m, sem_yn,
            sem_ym, sem_c, sem_l, sem_rs):
     rows, cols = x_ref.shape
     nt = rows // TB
@@ -71,25 +71,31 @@
             src_ref=source, dst_ref=target, send_sem=sem.at[(0, *index)], recv_sem=sem.at[(1, *index)],
             device_id=device, device_id_type=MESH)
 
-    for q in range(nt):
-        load(q).wait()
-        part = x_ref[q * TB:(q + 1) * TB, :]
-        part = part - jnp.sum(part, axis=1, keepdims=True) * (1.0 / cols)
-        xf[q * TB:(q + 1) * TB, :] = part
-        square = part[:, :128] * part[:, :128]
-        for s in range(1, cols // 128):
-            lanes = part[:, s * 128:(s + 1) * 128]
-            square = square + lanes * lanes
-        mine[q:q + 1, :] = jnp.sum(square.T, axis=0, keepdims=True)
-    mine[nt:, :] = jnp.zeros((8 - nt, 128), jnp.float32)
-    pl.semaphore_wait(barrier, 12)
-    for s, d in enumerate(peers):
-        copy(mine, sums.at[r], sem_sum, (s,), d).start()
-    total = mine[...]
-    for s, d in enumerate(peers):
-        copy(mine, sums.at[(r + 7 - s) % 8], sem_sum, (s,), d).wait_recv()
-        total = total + sums[(r + 7 - s) % 8]
-    scale = lax.rsqrt(total * (1.0 / entries) + 1e-05) * (1.0 / math.sqrt(entries))
+    half = nt // 2
+    for n in range(2):
+        for q in range(n * half, (n + 1) * half):
+            load(q).wait()
+            part = x_ref[q * TB:(q + 1) * TB, :]
+            part = part - jnp.sum(part, axis=1, keepdims=True) * (1.0 / cols)
+            xf[q * TB:(q + 1) * TB, :] = part
+            square = part[:, :128] * part[:, :128]
+            for s in range(1, cols // 128):
+                lanes = part[:, s * 128:(s + 1) * 128]
+                square = square + lanes * lanes
+            mine[n, q % half:q % half + 1, :] = jnp.sum(square.T, axis=0, keepdims=True)
+        mine[n, half:, :] = jnp.zeros((8 - half, 128), jnp.float32)
+        if n == 0:
+            pl.semaphore_wait(barrier, 12)
+        for s, d in enumerate(peers):
+            copy(mine.at[n], sums.at[r, n], sem_sum, (s, n), d).start()
+
+    def scales(n):
+        total = mine[n]
+        for s, d in enumerate(peers):
+            sender = (r + 7 - s) % 8
+            copy(mine.at[n], sums.at[sender, n], sem_sum, (s, n), d).wait_recv()
+            total = total + sums[sender, n]
+        return lax.rsqrt(total * (1.0 / entries) + 1e-05) * (1.0 / math.sqrt(entries))
 
     def at(t):
         return t * CH // TB, pl.ds(t * CH % TB, CH)
@@ -114,7 +120,9 @@
 
     native = jnp.where(src, 2 * k + zl, 4)
     for q in range(nt):
-        spread = jnp.broadcast_to(scale[q:q + 1, :], (128, 128)).T
+        if q % half == 0:
+            scale = scales(q // half)
+        spread = jnp.broadcast_to(scale[q % half:q % half + 1, :], (128, 128)).T
         rh, span = q * TB // RB, slice(q * TB % RB, q * TB % RB + TB)
         for s in range(cols // 128):
             lanes = slice(s * 128, (s + 1) * 128)
@@ -288,6 +296,10 @@
                 acc[e, h, t, rh] = acc[e, h, t, rh] + buf[t, rh]
                 c_rs(onward, t, rh).start()
 
+    def store(t, rh, h):
+        region = (pl.ds(rh * RB, RB), pl.ds((h * nt + t) * TB, TB))
+        return pltpu.make_async_copy(o_ref.at[region], o_hbm.at[region], sem_o.at[t, rh, h])
+
     def finish(a):
         t, rh = a
         for kind in (FP0, FP1, FM0, FM1):
@@ -295,6 +307,7 @@
         for h in range(2):
             lanes = slice((h * nt + t) * TB, (h * nt + t + 1) * TB)
             o_ref[rh * RB:(rh + 1) * RB, lanes] = acc[3, h, t, rh] + fp[h, t, rh] + fm[h, t, rh]
+            store(t, rh, h).start()
 
     stages = {
         "1": s1, "1n": s1n, "2a": lambda t: s2(t, first), "2b": lambda t: s2(t, 1 - first), "3o": s3o, "3a": s3a,
@@ -304,7 +317,8 @@
         stages[name](argument)
 
     for s, d in enumerate(peers):
-        copy(mine, sums.at[r], sem_sum, (s,), d).wait_send()
+        for n in range(2):
+            copy(mine.at[n], sums.at[r, n], sem_sum, (s, n), d).wait_send()
     for t in range(nc):
         @pl.when(src)
         def _():
@@ -327,6 +341,8 @@
                 c_c(t, j, kk).wait_send()
     for t in range(nt):
         for rh in range(2):
+            for h in range(2):
+                store(t, rh, h).wait()
             for kind in range(6):
                 c_rs(kind, t, rh).wait_send()
 
@@ -340,13 +356,15 @@
         functools.partial(kernel, entries),
         out_shape=jax.ShapeDtypeStruct((rows, 2 * rows), jnp.float32),
         in_specs=[pl.BlockSpec(memory_space=pl.ANY)],
-        out_specs=pl.BlockSpec(memory_space=pltpu.VMEM),
+        out_specs=pl.BlockSpec(memory_space=pl.ANY),
         scratch_shapes=[
             pltpu.VMEM((rows, cols), jnp.float32),
             dma((nt,)),
+            pltpu.VMEM((rows, 2 * rows), jnp.float32),
+            dma((nt, 2, 2)),
             pltpu.VMEM((rows, cols), jnp.float32),
-            pltpu.VMEM((8, 128), jnp.float32),
-            pltpu.VMEM((8, 8, 128), jnp.float32),
+            pltpu.VMEM((2, 8, 128), jnp.float32),
+            pltpu.VMEM((8, 2, 8, 128), jnp.float32),
             pltpu.VMEM((5, rows // RB, RB, cols), jnp.bfloat16),
             pltpu.VMEM((2, 2, nt, 2, TB, cols), jnp.bfloat16),
             pltpu.VMEM((4, 2, nt, rows // RB, RB, TB), jnp.float32),
@@ -354,7 +372,7 @@
             pltpu.VMEM((nt, rows // RB, RB, TB), jnp.float32),
             pltpu.VMEM((2, nt, rows // RB, RB, TB), jnp.float32),
             pltpu.VMEM((2, nt, rows // RB, RB, TB), jnp.float32),
-            dma((2, 7)),
+            dma((2, 7, 2)),
             dma((2, nc)),
             dma((2, nc, 2)),
             dma((2, nc, 2)),

time: 148 us -> 147 us (level)
  no operation moved by 1% of the time
where the time goes in v3:
time: 147 us
  Pallas kernels  144 us (98%)
  local copies, waits for them, and re-layouts  3.16 us (2%)
    pallas_call x1, Pallas kernels, per_device(): pl.pallas_call(functools.partial(kernel, entries), out_shape=jax.ShapeDty...  144 us
    unnamed x1, local copies, waits for them, and re-layouts  3.16 us

profile of v3, /device:TPU:17, one launch (start us, length us, event | category | flops | bytes accessed | tf_op | source)
XLA Modules:
  0.0 146.7 jit_solution(11174915024572103441)
XLA Ops:
  0.0 143.5 %shard_map.17 = f32[512,1024]{1,0:T(8,128)} custom-call(f32[512,1,1536]{2,1,0:T(1,128)} %x_hbm.1), custom_call_target="tpu_custom_call" | custom-call | tf_op jit(solution)/shard_map/pallas_call | solution.py:355
  143.6 3.2 %copy.3 = f32[512,1024]{1,0:T(8,128)} copy(f32[512,1024]{1,0:T(8,128)} %shard_map.17) | data formatting | bytes 4194304

commit v4 on v3

--- a/solution.py
+++ b/solution.py
@@ -383,7 +383,7 @@
             dma((2, 6, nt, rows // RB)),
         ],
         compiler_params=pltpu.CompilerParams(
-            collective_id=0, has_side_effects=True, vmem_limit_bytes=60 * 2**20
+            collective_id=0, has_side_effects=True, vmem_limit_bytes=46 * 2**20
         ),
     )(projections)
 

time: 147 us -> 149 us (1.014)
    pallas_call x1, Pallas kernels: 144 us -> 145 us  [per_device(): pl.pallas_call(functools.partial(kernel, entries), out_shape=jax.ShapeDty...]
    unnamed x1 -> x3, local copies, waits for them, and re-layouts: 3.16 us -> 3.21 us
where the time goes in v4:
time: 149 us
  Pallas kernels  145 us (97%)
  local copies, waits for them, and re-layouts  3.21 us (2%)
    pallas_call x1, Pallas kernels, per_device(): pl.pallas_call(functools.partial(kernel, entries), out_shape=jax.ShapeDty...  145 us
    unnamed x3, local copies, waits for them, and re-layouts  3.21 us

profile of v4, /device:TPU:17, one launch (start us, length us, event | category | flops | bytes accessed | tf_op | source)
XLA Modules:
  0.0 148.5 jit_solution(4172599423016629512)
XLA Ops:
  0.0 0.0 copy-start
  0.0 1.9 %copy-done = f32[512,1,1536]{2,1,0:T(1,128)S(1)} copy-done((f32[512,1,1536]{2,1,0:T(1,128)S(1)}, f32[512,1,1536]{2,1,0:T(1,128)}, u32[]{:S(2)}) %copy-start) | copy-done | bytes 3145752
  1.9 145.3 %shard_map.17 = f32[512,1024]{1,0:T(8,128)S(1)} custom-call(f32[512,1,1536]{2,1,0:T(1,128)S(1)} %copy-done), custom_call_target="tpu_custom_call" | custom-call | tf_op jit(solution)/shard_map/pallas_call | solution.py:355
  147.2 1.3 copy.3
Async XLA Ops:
  0.0 1.9 %copy-start = (f32[512,1,1536]{2,1,0:T(1,128)S(1)}, f32[512,1,1536]{2,1,0:T(1,128)}, u32[]{:S(2)}) copy-start(f32[512,1,1536]{2,1,0:T(1,128)} %x_hbm.1) | copy-start | bytes 9437188
